TPU v7x, 32 devices: a whole 2x2x4 slice. The times are simulated.
32 devices in a mesh: wide: 8 (over y, x, core), narrow: 4 (over z).
Axes of the slice: x: 2, y: 2, z: 4, core: 2. Of those that a mesh axis runs over, the one named last changes fastest.
Arguments:
- activity: bfloat16 [32, 8, 512, 512], P(('wide', 'narrow')), may hold values from 0 to 1
- tile_coords: int32 [32, 2], replicated, may hold values from 0 to 7, as said below
- user_owner: int32 [8], replicated, may hold values from 0 to 7, each once
- item_owner: int32 [8], replicated, may hold values from 0 to 7, each once
- user_factor: float32 [4096, 256], P('wide', 'narrow'), may hold values from 0 to 1
- item_factor: float32 [4096, 256], P('wide', 'narrow'), may hold values from 0 to 1
- time_factor: float32 [8, 256], replicated, may hold values from 0.0003 to 0.003
- user_dual: float32 [4096, 256], P('wide', 'narrow'), may hold values from -1.8 to 1.8
- item_dual: float32 [4096, 256], P('wide', 'narrow'), may hold values from -1.8 to 1.8
Outputs:
- new_users: float32 [4096, 256], P('wide', 'narrow')
- new_items: float32 [4096, 256], P('wide', 'narrow')
- new_user_dual: float32 [4096, 256], P('wide', 'narrow')
- new_item_dual: float32 [4096, 256], P('wide', 'narrow')
Inputs may be any that keep to these rules, and one draw needn't show every extreme that they name: `tile_coords`: no pair of blocks appears twice. `user_owner`: each stored row block holds exactly one user block. `item_owner`: each stored row block holds exactly one item block.
All inputs are finite; a program needn't handle non-finite values.
Results may differ from a plain program's by a relative error of at most 0.0017.
The roundings to bfloat16 on the way count: a program that leaves them out, or rounds other values in their place, can miss the bound.
Values may be sent and summed in bfloat16 or wider, within the bound.
No kernel may reach another device: no remote copies, remote signals or barrier semaphores. Data moves between devices by JAX's collectives and lax.ppermute only.
A program may use at most 64 MiB of HBM per device.

v0:
```python
import jax
import jax.numpy as jnp
from jax import lax
from jax.sharding import PartitionSpec as P

RANK = 256
BLOCK = 512
PASSES = 2


def locate(owner, wanted_blocks):
    everyone = jnp.arange(owner.shape[0], dtype=jnp.int32)
    chosen = jnp.where(everyone[None, :] == wanted_blocks[:, None], owner[None, :], 0)
    return jnp.sum(chosen, axis=1)


def fetch_rows(factor, wanted):
    lowered = factor.astype(jnp.bfloat16)
    width = factor.shape[1]
    slots = wanted.shape[0]
    initial = jnp.zeros((slots, BLOCK, width), jnp.bfloat16)
    portion = lax.all_gather(lowered, "wide", axis=0, tiled=True)
    count_blocks = portion.shape[0] // BLOCK
    shaped = portion.reshape(count_blocks, BLOCK, width)
    first = jnp.int32(0) // BLOCK
    onehot = (wanted[:, None] == first + jnp.arange(count_blocks, dtype=jnp.int32)[None, :]).astype(
        jnp.bfloat16
    )
    picked = jnp.einsum("jq,qrc->jrc", onehot, shaped, preferred_element_type=jnp.float32)
    gathered = initial + picked.astype(jnp.bfloat16)
    return lax.all_to_all(gathered, "narrow", split_axis=0, concat_axis=2, tiled=True)


def tile_sums(activity, fetched, time_factor, forward):
    khatri = (fetched.astype(jnp.float32)[:, None] * time_factor[None, :, None, :]).astype(
        jnp.bfloat16
    )
    if forward:
        return jnp.einsum("tkij,tkjr->tir", activity, khatri, preferred_element_type=jnp.float32)
    return jnp.einsum("tkij,tkir->tjr", activity, khatri, preferred_element_type=jnp.float32)


def owner_sums(partial_value, targets, owned):
    received = lax.all_to_all(partial_value, "narrow", split_axis=2, concat_axis=0, tiled=True)
    width = received.shape[2]
    count_blocks = owned * lax.axis_size("wide") // BLOCK
    onehot = (jnp.arange(count_blocks, dtype=jnp.int32)[:, None] == targets[None, :]).astype(
        jnp.float32
    )
    placed = jnp.einsum("qj,jrc->qrc", onehot, received, precision=lax.Precision.HIGHEST)
    return lax.psum_scatter(
        placed.reshape(owned * lax.axis_size("wide"), width),
        "wide",
        scatter_dimension=0,
        tiled=True,
    )


def joint_gram(other_rows, time_factor):
    local_gram = jnp.dot(other_rows.T, other_rows, precision=lax.Precision.HIGHEST)
    total = lax.psum(local_gram, ("wide", "narrow"))
    gram = total * jnp.dot(time_factor.T, time_factor, precision=lax.Precision.HIGHEST)
    penalty = jnp.trace(gram) / RANK
    identity = jnp.eye(RANK, dtype=jnp.float32)
    lower = jnp.linalg.cholesky(gram + penalty * identity)
    inverse = jax.scipy.linalg.cho_solve((lower, True), identity)
    return (penalty, inverse)


def update_rows(
    activity, other_cols, other_rows, factor, dual, wanted, targets, time_factor, forward, owned
):
    fetched = fetch_rows(other_cols, wanted)
    partial_value = tile_sums(activity, fetched, time_factor, forward)
    sums = owner_sums(partial_value, targets, owned)
    sums_rows = lax.all_to_all(sums, "narrow", split_axis=0, concat_axis=1, tiled=True)
    penalty, inverse = joint_gram(other_rows, time_factor)
    for _ in range(PASSES):
        target = jnp.dot(
            sums_rows + penalty * (factor + dual), inverse, precision=lax.Precision.HIGHEST
        )
        factor = jnp.maximum(target - dual, 0.0)
        dual = dual + factor - target
    factor_cols, dual_cols = (
        lax.all_to_all(factor, "narrow", split_axis=1, concat_axis=0, tiled=True),
        lax.all_to_all(dual, "narrow", split_axis=1, concat_axis=0, tiled=True),
    )
    return (factor_cols, dual_cols, factor)


def local(
    activity,
    tile_coords,
    user_owner,
    item_owner,
    user_factor,
    item_factor,
    time_factor,
    user_dual,
    item_dual,
):
    narrow_size = lax.axis_size("narrow")
    slots = narrow_size * activity.shape[0]
    group_coords = lax.dynamic_slice_in_dim(tile_coords, lax.axis_index("wide") * slots, slots, 0)
    user_pos = locate(user_owner, group_coords[:, 0])
    item_pos = locate(item_owner, group_coords[:, 1])
    owned = user_factor.shape[0]
    user_rows, udual_rows, item_rows, idual_rows = (
        lax.all_to_all(user_factor, "narrow", split_axis=0, concat_axis=1, tiled=True),
        lax.all_to_all(user_dual, "narrow", split_axis=0, concat_axis=1, tiled=True),
        lax.all_to_all(item_factor, "narrow", split_axis=0, concat_axis=1, tiled=True),
        lax.all_to_all(item_dual, "narrow", split_axis=0, concat_axis=1, tiled=True),
    )
    new_users, new_user_dual, fresh_rows = update_rows(
        activity,
        item_factor,
        item_rows,
        user_rows,
        udual_rows,
        item_pos,
        user_pos,
        time_factor,
        True,
        owned,
    )
    new_items, new_item_dual, _ = update_rows(
        activity,
        new_users,
        fresh_rows,
        item_rows,
        idual_rows,
        user_pos,
        item_pos,
        time_factor,
        False,
        owned,
    )
    return (new_users, new_items, new_user_dual, new_item_dual)


def solution(mesh):
    in_specs = (
        P(("wide", "narrow"), None, None, None),
        P(),
        P(),
        P(),
        P("wide", "narrow"),
        P("wide", "narrow"),
        P(),
        P("wide", "narrow"),
        P("wide", "narrow"),
    )
    out_specs = (P("wide", "narrow"), P("wide", "narrow"), P("wide", "narrow"), P("wide", "narrow"))
    return jax.shard_map(local, mesh=mesh, in_specs=in_specs, out_specs=out_specs, check_vma=False)
```

profile of v0, /device:TPU:0, one launch (start us, length us, event | category | flops | bytes accessed | tf_op | source)
XLA Modules:
  0.0 562.6 jit_solution(15027327676209226072)
XLA Ops:
  9.6 6.3 %all-to-all-start.3 = ((f32[4,128,64]{1,2,0:T(8,128)}), f32[4,128,64]{1,2,0:T(8,128)S(1)}, u32[]{:S(2)}, u32[]{:S(2)}) async-start(f32[4,128,64]{1,2,0:T(8,128)} %copy_bitcast_fusion.8), calls=%async_computation.4 | async-start | bytes 262144 | tf_op jit(solution)/shard_map/all_to_all | solution.py:111
  16.9 9.9 %all_gather.6 = bf16[4096,64]{0,1:T(8,128)(2,1)S(1)} all-gather(bf16[512,64]{0,1:T(8,128)(2,1)S(1)} %convert_element_type.70), channel_id=1, replica_groups=mesh['wide'=8,'narrow'=4] {'wide'}, dimensions={0}, use_global_device_ids=true | all-gather | bytes 589824 | tf_op jit(solution)/shard_map/all_gather | solution.py:22
  33.5 5.1 all-to-all-start.4
  39.7 5.3 all-to-all-done.4
  49.3 5.1 all-to-all-done.5
  57.8 116.1 %all-reduce.4.cloned.1.call-done = f32[256,256]{0,1:T(8,128)} async-done(((f32[256,256]{0,1:T(8,128)}), f32[256,256]{0,1:T(8,128)}) %all-reduce.4.cloned.1.call-update) | async-done | bytes 262160 | tf_op jit(solution)/shard_map/psum | solution.py:61
  176.8 11.7 %cholesky.130 = f32[128,128]{1,0:T(8,128)S(1)} custom-call(f32[128,128]{1,0:T(8,128)S(1)} %cholesky.194), custom_call_target="Cholesky" | custom-call | tf_op jit(solution)/shard_map/jit(cholesky)/cholesky | solution.py:65
  188.6 9.8 %custom-call.15 = f32[1,128,128]{1,2,0:T(8,128)S(1)} custom-call(f32[1,128,128]{2,1,0:T(8,128)S(1)} %get-tuple-element.59), custom_call_target="InvertDiagBlocksLowerTriangular" | custom-call | tf_op jit(solution)/shard_map/jit(cholesky)/cholesky | solution.py:65
  203.5 3.6 all-to-all-start.1
  207.8 11.7 %cholesky.147 = f32[128,128]{1,0:T(8,128)S(1)} custom-call(f32[128,128]{1,0:T(8,128)S(1)} %convolution_subtract_fusion.5), custom_call_target="Cholesky" | custom-call | tf_op jit(solution)/shard_map/jit(cholesky)/cholesky | solution.py:65
  224.3 4.0 while.4
  228.3 19.7 %custom-call.16 = f32[2,128,128]{1,2,0:T(8,128)S(1)} custom-call(f32[2,128,128]{2,1,0:T(8,128)S(1)} %get-tuple-element.20), custom_call_target="InvertDiagBlocksLowerTriangular" | custom-call | tf_op jit(solution)/shard_map/jit(_cho_solve)/triangular_solve | solution.py:66
  249.6 12.0 %reduce-scatter.3.cloned.1.call-done = f32[512,64]{0,1:T(8,128)} async-done(((f32[4096,64]{0,1:T(8,128)}), f32[512,64]{0,1:T(8,128)}) %reduce-scatter.3.cloned.1.call-update) | async-done | bytes 131088 | tf_op jit(solution)/shard_map/reduce_scatter | solution.py:51
  263.2 4.6 all-to-all-start.2
  268.1 5.7 %all-to-all-done.2 = f32[4,128,64]{1,2,0:T(8,128)S(1)} async-done(((f32[4,128,64]{1,2,0:T(8,128)}), f32[4,128,64]{1,2,0:T(8,128)S(1)}, u32[]{:S(2)}, u32[]{:S(2)}) %all-to-all-start.2) | async-done | bytes 131104 | tf_op jit(solution)/shard_map/all_to_all | solution.py:76
  279.1 3.9 all-to-all-done.10
  287.9 122.6 %all-reduce.6.cloned.1.call-done = f32[256,256]{0,1:T(8,128)} async-done(((f32[256,256]{0,1:T(8,128)}), f32[256,256]{0,1:T(8,128)}) %all-reduce.6.cloned.1.call-update) | async-done | bytes 262160 | tf_op jit(solution)/shard_map/psum | solution.py:61
  413.6 10.0 %all_gather.7 = bf16[4096,64]{0,1:T(8,128)(2,1)S(1)} all-gather(bf16[512,64]{0,1:T(8,128)(2,1)S(1)} %get-tuple-element.40), channel_id=1, replica_groups=mesh['wide'=8,'narrow'=4] {'wide'}, dimensions={0}, use_global_device_ids=true | all-gather | bytes 589824 | tf_op jit(solution)/shard_map/all_gather | solution.py:22
  424.9 3.6 all-to-all-start.7
  428.5 11.7 %cholesky.164 = f32[128,128]{1,0:T(8,128)S(1)} custom-call(f32[128,128]{1,0:T(8,128)S(1)} %cholesky.197), custom_call_target="Cholesky" | custom-call | tf_op jit(solution)/shard_map/jit(cholesky)/cholesky | solution.py:65
  440.3 9.8 %custom-call.17 = f32[1,128,128]{1,2,0:T(8,128)S(1)} custom-call(f32[1,128,128]{2,1,0:T(8,128)S(1)} %get-tuple-element.55), custom_call_target="InvertDiagBlocksLowerTriangular" | custom-call | tf_op jit(solution)/shard_map/jit(cholesky)/cholesky | solution.py:65
  450.4 3.5 fusion.11
  455.2 5.1 all-to-all-start.8
  460.8 11.7 %cholesky.181 = f32[128,128]{1,0:T(8,128)S(1)} custom-call(f32[128,128]{1,0:T(8,128)S(1)} %convolution_subtract_fusion.4), custom_call_target="Cholesky" | custom-call | tf_op jit(solution)/shard_map/jit(cholesky)/cholesky | solution.py:65
  477.9 4.0 while.5
  481.9 19.7 %custom-call.18 = f32[2,128,128]{1,2,0:T(8,128)S(1)} custom-call(f32[2,128,128]{2,1,0:T(8,128)S(1)} %get-tuple-element.21), custom_call_target="InvertDiagBlocksLowerTriangular" | custom-call | tf_op jit(solution)/shard_map/jit(_cho_solve)/triangular_solve | solution.py:66
  503.2 11.4 %reduce-scatter.5.cloned.1.call-done = f32[512,64]{0,1:T(8,128)} async-done(((f32[4096,64]{0,1:T(8,128)}), f32[512,64]{0,1:T(8,128)}) %reduce-scatter.5.cloned.1.call-update) | async-done | bytes 131088 | tf_op jit(solution)/shard_map/reduce_scatter | solution.py:51
  516.1 4.6 all-to-all-start.9
  521.0 5.7 %all-to-all-done.9 = f32[4,128,64]{1,2,0:T(8,128)S(1)} async-done(((f32[4,128,64]{1,2,0:T(8,128)}), f32[4,128,64]{1,2,0:T(8,128)S(1)}, u32[]{:S(2)}, u32[]{:S(2)}) %all-to-all-start.9) | async-done | bytes 131104 | tf_op jit(solution)/shard_map/all_to_all | solution.py:76
  531.4 4.4 all-to-all-done.12
  540.6 4.5 all-to-all-done.11
  549.1 5.2 all-to-all-done.13
  (127 shorter events, 78.5 us)
Async XLA Ops:
  8.0 19.7 %copy-start = (f32[512,64]{0,1:T(8,128)S(1)}, f32[512,64]{0,1:T(8,128)}, u32[]{:S(2)}) copy-start(f32[512,64]{0,1:T(8,128)} %param.16) | copy-start | bytes 393220
  8.0 165.9 %copy-start.1 = (f32[8,256]{1,0:T(8,128)S(1)}, f32[8,256]{1,0:T(8,128)}, u32[]{:S(2)}) copy-start(f32[8,256]{1,0:T(8,128)} %param.18) | copy-start | bytes 24580
  9.6 23.9 %all-to-all-start.3 = ((f32[4,128,64]{1,2,0:T(8,128)}), f32[4,128,64]{1,2,0:T(8,128)S(1)}, u32[]{:S(2)}, u32[]{:S(2)}) async-start(f32[4,128,64]{1,2,0:T(8,128)} %copy_bitcast_fusion.8), calls=%async_computation.4 | async-start | bytes 262144 | tf_op jit(solution)/shard_map/all_to_all | solution.py:111
  33.5 11.5 %all-to-all-start.4 = ((f32[4,128,64]{1,2,0:T(8,128)}), f32[4,128,64]{1,2,0:T(8,128)S(1)}, u32[]{:S(2)}, u32[]{:S(2)}) async-start(f32[4,128,64]{1,2,0:T(8,128)} %copy_bitcast_fusion.7), calls=%async_computation.5 | async-start | bytes 262144 | tf_op jit(solution)/shard_map/all_to_all | solution.py:109
  38.6 135.3 %all-reduce.4.cloned.1.call-start = ((), (), s32[]{:S(2)}) async-start(), calls=%async_computation.17 | async-start | bytes 524288 | tf_op jit(solution)/shard_map/psum | solution.py:61
  45.1 9.3 %all-to-all-start.5 = ((f32[4,128,64]{1,2,0:T(8,128)}), f32[4,128,64]{1,2,0:T(8,128)S(1)}, u32[]{:S(2)}, u32[]{:S(2)}) async-start(f32[4,128,64]{1,2,0:T(8,128)} %copy_bitcast_fusion.6), calls=%async_computation.6 | async-start | bytes 262144 | tf_op jit(solution)/shard_map/all_to_all | solution.py:110
  54.3 144.3 %all-to-all-start = ((bf16[4,512,64]{1,2,0:T(8,128)(2,1)}), bf16[4,512,64]{1,2,0:T(8,128)(2,1)S(1)}, u32[]{:S(2)}, u32[]{:S(2)}) async-start(bf16[4,512,64]{1,2,0:T(8,128)(2,1)} %copy.173), calls=%async_computation | async-start | bytes 524288 | tf_op jit(solution)/shard_map/all_to_all | solution.py:31
  203.5 18.1 %all-to-all-start.1 = ((f32[1,512,256]{1,0,2:T(1,128)}), f32[1,512,256]{1,0,2:T(1,128)S(1)}, u32[]{:S(2)}, u32[]{:S(2)}) async-start(f32[1,512,256]{1,0,2:T(1,128)} %copy.174), calls=%async_computation.1 | async-start | bytes 1048576 | tf_op jit(solution)/shard_map/all_to_all | solution.py:44
  207.1 54.6 %reduce-scatter.3.cloned.1.call-start = ((), (), s32[]{:S(2)}) async-start(), calls=%async_computation.16 | async-start | bytes 1179648 | tf_op jit(solution)/shard_map/reduce_scatter | solution.py:51
  263.2 10.5 %all-to-all-start.2 = ((f32[4,128,64]{1,2,0:T(8,128)}), f32[4,128,64]{1,2,0:T(8,128)S(1)}, u32[]{:S(2)}, u32[]{:S(2)}) async-start(f32[4,128,64]{1,2,0:T(8,128)} %copy_bitcast_fusion.9), calls=%async_computation.3 | async-start | bytes 262144 | tf_op jit(solution)/shard_map/all_to_all | solution.py:76
  273.7 9.2 %all-to-all-start.10 = ((f32[4,128,64]{1,2,0:T(8,128)}), f32[4,128,64]{1,2,0:T(8,128)S(1)}, u32[]{:S(2)}, u32[]{:S(2)}) async-start(f32[4,128,64]{1,2,0:T(8,128)} %copy_bitcast_fusion.4), calls=%async_computation.12 | async-start | bytes 262144 | tf_op jit(solution)/shard_map/all_to_all | solution.py:112
  277.1 133.4 %all-reduce.6.cloned.1.call-start = ((), (), s32[]{:S(2)}) async-start(), calls=%async_computation.19 | async-start | bytes 524288 | tf_op jit(solution)/shard_map/psum | solution.py:61
  283.8 129.1 %all-to-all-start.6 = ((f32[128,4,64]{0,2,1:T(8,128)}), f32[128,4,64]{0,2,1:T(8,128)S(1)}, u32[]{:S(2)}, u32[]{:S(2)}) async-start(f32[128,4,64]{0,2,1:T(8,128)} %bitcast.28), calls=%async_computation.7 | async-start | bytes 262144 | tf_op jit(solution)/shard_map/all_to_all | solution.py:85
  424.9 25.5 %all-to-all-start.7 = ((bf16[4,512,64]{1,2,0:T(8,128)(2,1)}), bf16[4,512,64]{1,2,0:T(8,128)(2,1)S(1)}, u32[]{:S(2)}, u32[]{:S(2)}) async-start(bf16[4,512,64]{1,2,0:T(8,128)(2,1)} %copy.192), calls=%async_computation.8 | async-start | bytes 524288 | tf_op jit(solution)/shard_map/all_to_all | solution.py:31
  455.2 20.0 %all-to-all-start.8 = ((f32[1,512,256]{1,0,2:T(1,128)}), f32[1,512,256]{1,0,2:T(1,128)S(1)}, u32[]{:S(2)}, u32[]{:S(2)}) async-start(f32[1,512,256]{1,0,2:T(1,128)} %copy.193), calls=%async_computation.9 | async-start | bytes 1048576 | tf_op jit(solution)/shard_map/all_to_all | solution.py:44
  460.3 54.2 %reduce-scatter.5.cloned.1.call-start = ((), (), s32[]{:S(2)}) async-start(), calls=%async_computation.18 | async-start | bytes 1179648 | tf_op jit(solution)/shard_map/reduce_scatter | solution.py:51
  516.1 10.5 %all-to-all-start.9 = ((f32[4,128,64]{1,2,0:T(8,128)}), f32[4,128,64]{1,2,0:T(8,128)S(1)}, u32[]{:S(2)}, u32[]{:S(2)}) async-start(f32[4,128,64]{1,2,0:T(8,128)} %copy_bitcast_fusion.5), calls=%async_computation.11 | async-start | bytes 262144 | tf_op jit(solution)/shard_map/all_to_all | solution.py:76
  526.6 9.2 %all-to-all-start.12 = ((f32[128,4,64]{0,2,1:T(8,128)}), f32[128,4,64]{0,2,1:T(8,128)S(1)}, u32[]{:S(2)}, u32[]{:S(2)}) async-start(f32[128,4,64]{0,2,1:T(8,128)} %bitcast.54), calls=%async_computation.14 | async-start | bytes 262144 | tf_op jit(solution)/shard_map/all_to_all | solution.py:86
  535.9 9.2 %all-to-all-start.11 = ((f32[128,4,64]{0,2,1:T(8,128)}), f32[128,4,64]{0,2,1:T(8,128)S(1)}, u32[]{:S(2)}, u32[]{:S(2)}) async-start(f32[128,4,64]{0,2,1:T(8,128)} %bitcast.52), calls=%async_computation.13 | async-start | bytes 262144 | tf_op jit(solution)/shard_map/all_to_all | solution.py:85
  545.1 9.2 %all-to-all-start.13 = ((f32[128,4,64]{0,2,1:T(8,128)}), f32[128,4,64]{0,2,1:T(8,128)S(1)}, u32[]{:S(2)}, u32[]{:S(2)}) async-start(f32[128,4,64]{0,2,1:T(8,128)} %bitcast.56), calls=%async_computation.15 | async-start | bytes 262144 | tf_op jit(solution)/shard_map/all_to_all | solution.py:86
Sparse Core Ops, SparseCore 0:
  44.9 128.9 all-reduce.3
  283.4 127.0 all-reduce.5
Sparse Core Ops, SparseCore 1:
  224.3 37.3 reduce-scatter.2
  477.9 36.6 reduce-scatter.4
where the time goes:
time: 572 us; the launch traced here: 563 us
  waiting for transfers between devices  302 us (53%)
  other arithmetic  113 us (20%)
  starting transfers between devices  57 us (10%)
  local copies, waits for them, and re-layouts  30.9 us (5%)
  between operations  20.2 us (4%)
  blocking collectives  19.8 us (3%)
  matrix products  19.7 us (3%)
    psum x2, waiting for transfers between devices, joint_gram(): total = lax.psum(local_gram, ('wide', 'narrow'))  239 us
    another operation x13, other arithmetic, joint_gram(): lower = jnp.linalg.cholesky(gram + penalty * identity)  68.5 us
    another operation x5, other arithmetic, joint_gram(): inverse = jax.scipy.linalg.cho_solve((lower, True), identity)  39.4 us
    reduce_scatter x2, waiting for transfers between devices, owner_sums(): lax.psum_scatter(placed.reshape(owned * lax.axis_size('wide'), width), 'w...  23.4 us
    all_gather x2, blocking collectives, fetch_rows(): portion = lax.all_gather(lowered, 'wide', axis=0, tiled=True)  19.8 us
  transfers between devices with their start and end apart: 18, of which 12 were waited for; matrix products, arithmetic and copies ran while one was open for 25% of the time, Pallas kernels for 0%

commit v1 on v0

--- a/solution.py
+++ b/solution.py
@@ -58,7 +58,7 @@
 
 def joint_gram(other_rows, time_factor):
     local_gram = jnp.dot(other_rows.T, other_rows, precision=lax.Precision.HIGHEST)
-    total = lax.psum(local_gram, ("wide", "narrow"))
+    total = jnp.sum(jax.lax.all_gather(local_gram, ("wide", "narrow")), axis=0)
     gram = total * jnp.dot(time_factor.T, time_factor, precision=lax.Precision.HIGHEST)
     penalty = jnp.trace(gram) / RANK
     identity = jnp.eye(RANK, dtype=jnp.float32)

time: 572 us -> 453 us (0.79)
  waiting for transfers between devices: 302 us -> 148 us
  blocking collectives: 19.8 us -> 82 us
  starting transfers between devices: 57 us -> 34.6 us
  other arithmetic: 113 us -> 120 us
    psum x2 -> x0, waiting for transfers between devices: 239 us -> none  [joint_gram(): total = lax.psum(local_gram, ('wide', 'narrow'))]
    all_to_all x0 -> x5, blocking collectives: none -> 60.9 us  [the longest x2 26.1 us: fetch_rows(): lax.all_to_all(gathered, 'narrow', split_axis=0, concat_axis=2, tiled=True)]
    all_gather x0 -> x2, waiting for transfers between devices: none -> 58.6 us  [joint_gram(): total = jnp.sum(jax.lax.all_gather(local_gram, ('wide', 'narrow')), axis=0)]
    reduce_scatter x2, waiting for transfers between devices: 23.4 us -> 46.7 us  [owner_sums(): lax.psum_scatter(placed.reshape(owned * lax.axis_size('wide'), width), 'w...]
    all_to_all x3 -> x0, starting transfers between devices: 13.4 us -> none  [the longest x2 7.03 us: fetch_rows(): lax.all_to_all(gathered, 'narrow', split_axis=0, concat_axis=2, tiled=True)]
    all_to_all x2 -> x1, waiting for transfers between devices: 0.01 us -> 13.1 us  [owner_sums(): lax.all_to_all(partial_value, 'narrow', split_axis=2, concat_axis=0, tile...]
    reduce_sum x0 -> x2, other arithmetic: none -> 7.86 us  [joint_gram(): total = jnp.sum(jax.lax.all_gather(local_gram, ('wide', 'narrow')), axis=0)]
  transfers between devices with their start and end apart: 18 -> 13, of which waited for: 12 -> 10; matrix products, arithmetic and copies ran while one was open for 25% -> 18% of each run, Pallas kernels for 0% -> 0%
where the time goes in v1:
time: 453 us; the launch traced here: 446 us
  waiting for transfers between devices  148 us (33%)
  other arithmetic  120 us (26%)
  blocking collectives  82 us (18%)
  starting transfers between devices  34.6 us (8%)
  local copies, waits for them, and re-layouts  25.2 us (6%)
  between operations  20.4 us (5%)
  matrix products  16.5 us (4%)
    another operation x13, other arithmetic, joint_gram(): lower = jnp.linalg.cholesky(gram + penalty * identity)  68.6 us
    all_gather x2, waiting for transfers between devices, joint_gram(): total = jnp.sum(jax.lax.all_gather(local_gram, ('wide', 'narrow')), axis=0)  58.6 us
    reduce_scatter x2, waiting for transfers between devices, owner_sums(): lax.psum_scatter(placed.reshape(owned * lax.axis_size('wide'), width), 'w...  46.7 us
    another operation x5, other arithmetic, joint_gram(): inverse = jax.scipy.linalg.cho_solve((lower, True), identity)  39.7 us
    all_to_all x2, blocking collectives, fetch_rows(): lax.all_to_all(gathered, 'narrow', split_axis=0, concat_axis=2, tiled=True)  26.1 us
    all_gather x2, blocking collectives, fetch_rows(): portion = lax.all_gather(lowered, 'wide', axis=0, tiled=True)  21.1 us
    all_to_all x1, blocking collectives, owner_sums(): lax.all_to_all(partial_value, 'narrow', split_axis=2, concat_axis=0, tile...  16.7 us
    all_to_all x2, waiting for transfers between devices, update_rows(): lax.all_to_all(sums, 'narrow', split_axis=0, concat_axis=1, tiled=True)  13.7 us
  transfers between devices with their start and end apart: 13, of which 10 were waited for; matrix products, arithmetic and copies ran while one was open for 18% of the time, Pallas kernels for 0%

profile of v1, /device:TPU:0, one launch (start us, length us, event | category | flops | bytes accessed | tf_op | source)
XLA Modules:
  0.0 446.4 jit_solution(10180100401966581816)
XLA Ops:
  9.0 11.3 %all_gather.18 = bf16[4096,64]{0,1:T(8,128)(2,1)S(1)} all-gather(bf16[512,64]{0,1:T(8,128)(2,1)S(1)} %convert_element_type.70), channel_id=1, replica_groups=mesh['wide'=8,'narrow'=4] {'wide'}, dimensions={0}, use_global_device_ids=true | all-gather | bytes 589824 | tf_op jit(solution)/shard_map/all_gather | solution.py:22
  22.5 14.1 %all_to_all.244 = bf16[4,512,64]{1,2,0:T(8,128)(2,1)S(1)} all-to-all(bf16[4,512,64]{1,2,0:T(8,128)(2,1)S(1)} %copy.167), channel_id=1, replica_groups=mesh['wide'=8,'narrow'=4] {'narrow'}, dimensions={0} | all-to-all | bytes 524288 | tf_op jit(solution)/shard_map/all_to_all | solution.py:31
  45.3 13.1 %all-to-all-done.1 = f32[1,512,256]{1,0,2:T(1,128)S(1)} async-done(((f32[1,512,256]{1,0,2:T(1,128)}), f32[1,512,256]{1,0,2:T(1,128)S(1)}, u32[]{:S(2)}, u32[]{:S(2)}) %all-to-all-start.1) | async-done | bytes 524320 | tf_op jit(solution)/shard_map/all_to_all | solution.py:44
  61.3 8.5 %all_to_all.245 = f32[4,128,64]{1,2,0:T(8,128)S(1)} all-to-all(f32[4,128,64]{1,2,0:T(8,128)S(1)} %copy_bitcast_fusion.8), channel_id=1, replica_groups=mesh['wide'=8,'narrow'=4] {'narrow'}, dimensions={0} | all-to-all | bytes 262144 | tf_op jit(solution)/shard_map/all_to_all | solution.py:111
  75.5 5.3 %all-to-all-done.4 = f32[4,128,64]{1,2,0:T(8,128)S(1)} async-done(((f32[4,128,64]{1,2,0:T(8,128)}), f32[4,128,64]{1,2,0:T(8,128)S(1)}, u32[]{:S(2)}, u32[]{:S(2)}) %all-to-all-start.4) | async-done | bytes 131104 | tf_op jit(solution)/shard_map/all_to_all | solution.py:109
  84.2 11.9 %reduce-scatter.3.cloned.1.call-done = f32[512,64]{0,1:T(8,128)} async-done(((f32[4096,64]{0,1:T(8,128)}), f32[512,64]{0,1:T(8,128)}) %reduce-scatter.3.cloned.1.call-update) | async-done | bytes 131088 | tf_op jit(solution)/shard_map/reduce_scatter | solution.py:51
  97.6 4.6 %all-to-all-start.2 = ((f32[4,128,64]{1,2,0:T(8,128)}), f32[4,128,64]{1,2,0:T(8,128)S(1)}, u32[]{:S(2)}, u32[]{:S(2)}) async-start(f32[4,128,64]{1,2,0:T(8,128)} %copy_bitcast_fusion.9), calls=%async_computation.3 | async-start | bytes 262144 | tf_op jit(solution)/shard_map/all_to_all | solution.py:76
  103.0 8.8 %all-to-all-done.2 = f32[4,128,64]{1,2,0:T(8,128)S(1)} async-done(((f32[4,128,64]{1,2,0:T(8,128)}), f32[4,128,64]{1,2,0:T(8,128)S(1)}, u32[]{:S(2)}, u32[]{:S(2)}) %all-to-all-start.2) | async-done | bytes 131104 | tf_op jit(solution)/shard_map/all_to_all | solution.py:76
  111.9 35.5 %all-gather.5.cloned.1.call-done = f32[8192,256]{1,0:T(8,128)} async-done(((f32[256,256]{1,0:T(8,128)}), f32[8192,256]{1,0:T(8,128)}) %all-gather.5.cloned.1.call-update) | async-done | bytes 8388624 | tf_op jit(solution)/shard_map/all_gather | solution.py:61
  147.3 3.9 reduce_sum.54
  153.3 11.7 %cholesky.130 = f32[128,128]{1,0:T(8,128)S(1)} custom-call(f32[128,128]{1,0:T(8,128)S(1)} %cholesky.194), custom_call_target="Cholesky" | custom-call | tf_op jit(solution)/shard_map/jit(cholesky)/cholesky | solution.py:65
  165.1 9.8 %custom-call.15 = f32[1,128,128]{1,2,0:T(8,128)S(1)} custom-call(f32[1,128,128]{2,1,0:T(8,128)S(1)} %get-tuple-element.59), custom_call_target="InvertDiagBlocksLowerTriangular" | custom-call | tf_op jit(solution)/shard_map/jit(cholesky)/cholesky | solution.py:65
  175.4 11.7 %cholesky.147 = f32[128,128]{1,0:T(8,128)S(1)} custom-call(f32[128,128]{1,0:T(8,128)S(1)} %convolution_subtract_fusion.5), custom_call_target="Cholesky" | custom-call | tf_op jit(solution)/shard_map/jit(cholesky)/cholesky | solution.py:65
  189.2 4.2 while.4
  193.4 19.7 %custom-call.16 = f32[2,128,128]{1,2,0:T(8,128)S(1)} custom-call(f32[2,128,128]{2,1,0:T(8,128)S(1)} %get-tuple-element.20), custom_call_target="InvertDiagBlocksLowerTriangular" | custom-call | tf_op jit(solution)/shard_map/jit(_cho_solve)/triangular_solve | solution.py:66
  215.6 9.6 %all_to_all.246 = f32[128,4,64]{0,2,1:T(8,128)S(1)} all-to-all(f32[128,4,64]{0,2,1:T(8,128)S(1)} %bitcast.257), channel_id=1, replica_groups=mesh['wide'=8,'narrow'=4] {'narrow'}, dimensions={1} | all-to-all | bytes 262144 | tf_op jit(solution)/shard_map/all_to_all | solution.py:85
  225.9 9.8 %all_gather.21 = bf16[4096,64]{0,1:T(8,128)(2,1)S(1)} all-gather(bf16[512,64]{0,1:T(8,128)(2,1)S(1)} %get-tuple-element.40), channel_id=1, replica_groups=mesh['wide'=8,'narrow'=4] {'wide'}, dimensions={0}, use_global_device_ids=true | all-gather | bytes 589824 | tf_op jit(solution)/shard_map/all_gather | solution.py:22
  236.3 12.1 %all_to_all.247 = bf16[4,512,64]{1,2,0:T(8,128)(2,1)S(1)} all-to-all(bf16[4,512,64]{1,2,0:T(8,128)(2,1)S(1)} %copy.186), channel_id=1, replica_groups=mesh['wide'=8,'narrow'=4] {'narrow'}, dimensions={0} | all-to-all | bytes 524288 | tf_op jit(solution)/shard_map/all_to_all | solution.py:31
  250.3 16.7 %all_to_all.248 = f32[1,512,256]{1,0,2:T(1,128)S(1)} all-to-all(f32[1,512,256]{1,0,2:T(1,128)S(1)} %copy.187), channel_id=1, replica_groups=mesh['wide'=8,'narrow'=4] {'narrow'}, dimensions={2} | all-to-all | bytes 1048576 | tf_op jit(solution)/shard_map/all_to_all | solution.py:44
  274.9 34.8 %reduce-scatter.5.cloned.1.call-done = f32[512,64]{0,1:T(8,128)} async-done(((f32[4096,64]{0,1:T(8,128)}), f32[512,64]{0,1:T(8,128)}) %reduce-scatter.5.cloned.1.call-update) | async-done | bytes 131088 | tf_op jit(solution)/shard_map/reduce_scatter | solution.py:51
  311.3 4.6 %all-to-all-start.9 = ((f32[4,128,64]{1,2,0:T(8,128)}), f32[4,128,64]{1,2,0:T(8,128)S(1)}, u32[]{:S(2)}, u32[]{:S(2)}) async-start(f32[4,128,64]{1,2,0:T(8,128)} %copy_bitcast_fusion.5), calls=%async_computation.11 | async-start | bytes 262144 | tf_op jit(solution)/shard_map/all_to_all | solution.py:76
  316.9 5.0 %all-to-all-done.9 = f32[4,128,64]{1,2,0:T(8,128)S(1)} async-done(((f32[4,128,64]{1,2,0:T(8,128)}), f32[4,128,64]{1,2,0:T(8,128)S(1)}, u32[]{:S(2)}, u32[]{:S(2)}) %all-to-all-start.9) | async-done | bytes 131104 | tf_op jit(solution)/shard_map/all_to_all | solution.py:76
  321.9 4.5 %all-to-all-start.12 = ((f32[128,4,64]{0,2,1:T(8,128)}), f32[128,4,64]{0,2,1:T(8,128)S(1)}, u32[]{:S(2)}, u32[]{:S(2)}) async-start(f32[128,4,64]{0,2,1:T(8,128)} %bitcast.56), calls=%async_computation.14 | async-start | bytes 262144 | tf_op jit(solution)/shard_map/all_to_all | solution.py:86
  326.5 23.2 %all-gather.7.cloned.1.call-done = f32[8192,256]{1,0:T(8,128)} async-done(((f32[256,256]{1,0:T(8,128)}), f32[8192,256]{1,0:T(8,128)}) %all-gather.7.cloned.1.call-update) | async-done | bytes 8388624 | tf_op jit(solution)/shard_map/all_gather | solution.py:61
  349.7 3.9 reduce_sum.56
  355.2 11.7 %cholesky.164 = f32[128,128]{1,0:T(8,128)S(1)} custom-call(f32[128,128]{1,0:T(8,128)S(1)} %cholesky.197), custom_call_target="Cholesky" | custom-call | tf_op jit(solution)/shard_map/jit(cholesky)/cholesky | solution.py:65
  367.0 9.8 %custom-call.17 = f32[1,128,128]{1,2,0:T(8,128)S(1)} custom-call(f32[1,128,128]{2,1,0:T(8,128)S(1)} %get-tuple-element.55), custom_call_target="InvertDiagBlocksLowerTriangular" | custom-call | tf_op jit(solution)/shard_map/jit(cholesky)/cholesky | solution.py:65
  377.3 11.7 %cholesky.181 = f32[128,128]{1,0:T(8,128)S(1)} custom-call(f32[128,128]{1,0:T(8,128)S(1)} %convolution_subtract_fusion.4), custom_call_target="Cholesky" | custom-call | tf_op jit(solution)/shard_map/jit(cholesky)/cholesky | solution.py:65
  391.8 4.1 while.5
  395.9 19.9 %custom-call.18 = f32[2,128,128]{1,2,0:T(8,128)S(1)} custom-call(f32[2,128,128]{2,1,0:T(8,128)S(1)} %get-tuple-element.21), custom_call_target="InvertDiagBlocksLowerTriangular" | custom-call | tf_op jit(solution)/shard_map/jit(_cho_solve)/triangular_solve | solution.py:66
  423.9 5.0 %all-to-all-done.11 = f32[128,4,64]{0,2,1:T(8,128)S(1)} async-done(((f32[128,4,64]{0,2,1:T(8,128)}), f32[128,4,64]{0,2,1:T(8,128)S(1)}, u32[]{:S(2)}, u32[]{:S(2)}) %all-to-all-start.11) | async-done | bytes 131104 | tf_op jit(solution)/shard_map/all_to_all | solution.py:85
  432.9 5.2 %all-to-all-done.13 = f32[128,4,64]{0,2,1:T(8,128)S(1)} async-done(((f32[128,4,64]{0,2,1:T(8,128)}), f32[128,4,64]{0,2,1:T(8,128)S(1)}, u32[]{:S(2)}, u32[]{:S(2)}) %all-to-all-start.13) | async-done | bytes 131104 | tf_op jit(solution)/shard_map/all_to_all | solution.py:86
  (136 shorter events, 68.4 us)
Async XLA Ops:
  8.0 62.9 %copy-start = (f32[512,64]{0,1:T(8,128)S(1)}, f32[512,64]{0,1:T(8,128)}, u32[]{:S(2)}) copy-start(f32[512,64]{0,1:T(8,128)} %param.16) | copy-start | bytes 393220
  8.0 28.6 %copy-start.4 = (f32[8,256]{1,0:T(8,128)S(1)}, f32[8,256]{1,0:T(8,128)}, u32[]{:S(2)}) copy-start(f32[8,256]{1,0:T(8,128)} %param.18) | copy-start | bytes 24580
  36.6 8.5 %copy-start.6 = (s32[8]{0:T(128)S(1)}, s32[8]{0:T(128)}, u32[]{:S(2)}) copy-start(s32[8]{0:T(128)} %param.14) | copy-start | bytes 100
  40.1 21.1 %copy-start.1 = (f32[512,64]{0,1:T(8,128)S(1)}, f32[512,64]{0,1:T(8,128)}, u32[]{:S(2)}) copy-start(f32[512,64]{0,1:T(8,128)} %param.17) | copy-start | bytes 393220
  41.5 33.4 %copy-start.2 = (f32[512,64]{0,1:T(8,128)S(1)}, f32[512,64]{0,1:T(8,128)}, u32[]{:S(2)}) copy-start(f32[512,64]{0,1:T(8,128)} %param.19) | copy-start | bytes 393220
  41.5 17.0 %all-to-all-start.1 = ((f32[1,512,256]{1,0,2:T(1,128)}), f32[1,512,256]{1,0,2:T(1,128)S(1)}, u32[]{:S(2)}, u32[]{:S(2)}) async-start(f32[1,512,256]{1,0,2:T(1,128)} %copy.168), calls=%async_computation.1 | async-start | bytes 1048576 | tf_op jit(solution)/shard_map/all_to_all | solution.py:44
  45.1 51.0 %reduce-scatter.3.cloned.1.call-start = ((), (), s32[]{:S(2)}) async-start(), calls=%async_computation.16 | async-start | bytes 1179648 | tf_op jit(solution)/shard_map/reduce_scatter | solution.py:51
  61.2 86.1 %all-gather.5.cloned.1.call-start = ((), (), s32[]{:S(2)}) async-start(), calls=%async_computation.18 | async-start | bytes 8650752 | tf_op jit(solution)/shard_map/all_gather | solution.py:61
  71.5 9.3 %all-to-all-start.4 = ((f32[4,128,64]{1,2,0:T(8,128)}), f32[4,128,64]{1,2,0:T(8,128)S(1)}, u32[]{:S(2)}, u32[]{:S(2)}) async-start(f32[4,128,64]{1,2,0:T(8,128)} %copy_bitcast_fusion.7), calls=%async_computation.5 | async-start | bytes 262144 | tf_op jit(solution)/shard_map/all_to_all | solution.py:109
  80.8 16.8 %all-to-all-start.5 = ((f32[4,128,64]{1,2,0:T(8,128)}), f32[4,128,64]{1,2,0:T(8,128)S(1)}, u32[]{:S(2)}, u32[]{:S(2)}) async-start(f32[4,128,64]{1,2,0:T(8,128)} %copy_bitcast_fusion.6), calls=%async_computation.6 | async-start | bytes 262144 | tf_op jit(solution)/shard_map/all_to_all | solution.py:110
  97.6 14.1 %all-to-all-start.2 = ((f32[4,128,64]{1,2,0:T(8,128)}), f32[4,128,64]{1,2,0:T(8,128)S(1)}, u32[]{:S(2)}, u32[]{:S(2)}) async-start(f32[4,128,64]{1,2,0:T(8,128)} %copy_bitcast_fusion.9), calls=%async_computation.3 | async-start | bytes 262144 | tf_op jit(solution)/shard_map/all_to_all | solution.py:76
  102.2 207.5 %reduce-scatter.5.cloned.1.call-start = ((), (), s32[]{:S(2)}) async-start(), calls=%async_computation.17 | async-start | bytes 1179648 | tf_op jit(solution)/shard_map/reduce_scatter | solution.py:51
  215.6 32.8 %copy-start.5 = (bf16[1,8,512,512]{3,2,1,0:T(8,128)(2,1)S(1)}, bf16[1,8,512,512]{3,2,1,0:T(8,128)(2,1)}, u32[]{:S(2)}) copy-start(bf16[1,8,512,512]{3,2,1,0:T(8,128)(2,1)} %param.12) | copy-start | bytes 12582916
  249.8 21.2 %copy-start.3 = (f32[512,64]{0,1:T(8,128)S(1)}, f32[512,64]{0,1:T(8,128)}, u32[]{:S(2)}) copy-start(f32[512,64]{0,1:T(8,128)} %param.20) | copy-start | bytes 393220
  269.7 79.9 %all-gather.7.cloned.1.call-start = ((), (), s32[]{:S(2)}) async-start(), calls=%async_computation.19 | async-start | bytes 8650752 | tf_op jit(solution)/shard_map/all_gather | solution.py:61
  271.6 39.7 %all-to-all-start.10 = ((f32[4,128,64]{1,2,0:T(8,128)}), f32[4,128,64]{1,2,0:T(8,128)S(1)}, u32[]{:S(2)}, u32[]{:S(2)}) async-start(f32[4,128,64]{1,2,0:T(8,128)} %copy_bitcast_fusion.4), calls=%async_computation.12 | async-start | bytes 262144 | tf_op jit(solution)/shard_map/all_to_all | solution.py:112
  311.3 10.5 %all-to-all-start.9 = ((f32[4,128,64]{1,2,0:T(8,128)}), f32[4,128,64]{1,2,0:T(8,128)S(1)}, u32[]{:S(2)}, u32[]{:S(2)}) async-start(f32[4,128,64]{1,2,0:T(8,128)} %copy_bitcast_fusion.5), calls=%async_computation.11 | async-start | bytes 262144 | tf_op jit(solution)/shard_map/all_to_all | solution.py:76
  321.9 97.3 %all-to-all-start.12 = ((f32[128,4,64]{0,2,1:T(8,128)}), f32[128,4,64]{0,2,1:T(8,128)S(1)}, u32[]{:S(2)}, u32[]{:S(2)}) async-start(f32[128,4,64]{0,2,1:T(8,128)} %bitcast.56), calls=%async_computation.14 | async-start | bytes 262144 | tf_op jit(solution)/shard_map/all_to_all | solution.py:86
  419.1 9.7 %all-to-all-start.11 = ((f32[128,4,64]{0,2,1:T(8,128)}), f32[128,4,64]{0,2,1:T(8,128)S(1)}, u32[]{:S(2)}, u32[]{:S(2)}) async-start(f32[128,4,64]{0,2,1:T(8,128)} %bitcast.54), calls=%async_computation.13 | async-start | bytes 262144 | tf_op jit(solution)/shard_map/all_to_all | solution.py:85
  428.9 9.2 %all-to-all-start.13 = ((f32[128,4,64]{0,2,1:T(8,128)}), f32[128,4,64]{0,2,1:T(8,128)S(1)}, u32[]{:S(2)}, u32[]{:S(2)}) async-start(f32[128,4,64]{0,2,1:T(8,128)} %bitcast.58), calls=%async_computation.15 | async-start | bytes 262144 | tf_op jit(solution)/shard_map/all_to_all | solution.py:86
Sparse Core Ops, SparseCore 0:
  61.3 34.6 reduce-scatter.2
  269.9 39.8 reduce-scatter.4
Sparse Core Ops, SparseCore 1:
  70.9 76.3 all-gather.4
  273.2 76.4 all-gather.6
